TPU v7x, 32 devices: a whole 2x2x4 slice. The times are simulated.
32 devices in a mesh: grp: 8 (over z, y), chan: 4 (over x, core).
Axes of the slice: x: 2, y: 2, z: 4, core: 2. Of those that a mesh axis runs over, the one named last changes fastest.
Arguments:
- grad_out: bfloat16 [64, 8, 16, 128], P('grp', 'chan'), may hold values from -6 to 6
- feat_full: bfloat16 [64, 8, 16, 128], P('grp', 'chan'), may hold values from -6 to 6
- filters_full: bfloat16 [3, 3, 3, 128, 128], replicated, may hold values from -0.109375 to 0.109375
- upsample_weight: bfloat16 [2, 2, 2, 512, 128], replicated, may hold values from -0.1875 to 0.1875
- filters_half: bfloat16 [3, 3, 3, 512, 512], P(None, None, None, None, 'chan'), may hold values from -0.0546875 to 0.0546875
Outputs:
- grad_half: bfloat16 [4, 32, 8, 512], P('chan', 'grp')
- taps_grad: float32 [3, 3, 3, 128, 128], P(None, None, None, 'grp', 'chan')
All inputs are finite; a program needn't handle non-finite values.
Results may differ from a plain program's by a relative error of at most 0.0058.
Values may be sent and summed in bfloat16 or wider, within the bound.
No kernel may reach another device: no remote copies, remote signals or barrier semaphores. Data moves between devices by JAX's collectives and lax.ppermute only.
A program may use at most 64 MiB of HBM per device.

v0:
```python
import jax
import jax.numpy as jnp
from jax import lax
from jax.sharding import PartitionSpec as P


def padded_2(cells, sides, width):
    for axis, dim in sides:
        count = lax.axis_size(axis)
        ends = count - 1
        head = lax.slice_in_dim(cells, 0, width, axis=dim)
        tail = lax.slice_in_dim(cells, cells.shape[dim] - width, cells.shape[dim], axis=dim)
        cells = jnp.concatenate(
            [
                lax.ppermute(tail, axis, [(i, (i + 1) % count) for i in range(ends)]),
                cells,
                lax.ppermute(head, axis, [((i + 1) % count, i) for i in range(ends)]),
            ],
            axis=dim,
        )
    return cells


def spread_taps(padded, weight, extent, summed, swapped):
    for p in range(3):
        for q in range(3):
            for r in range(3):
                window = padded[
                    2 - p : 2 - p + extent[0], 2 - q : 2 - q + extent[1], 2 - r : 2 - r + extent[2]
                ]
                kernel = weight[q, p, r] if swapped else weight[p, q, r]
                summed = summed + jnp.einsum(
                    "xyzo,io->xyzi", window, kernel, preferred_element_type=jnp.float32
                )
    return summed


def body(grad_out, feat_full, filters_full, upsample_weight, filters_half):
    extent = grad_out.shape[:3]
    channels = grad_out.shape[3]
    stacked = jnp.stack([grad_out, feat_full])
    bordered = padded_2(stacked, (("grp", 1), ("chan", 2)), 1)
    bordered = jnp.pad(bordered, ((0, 0), (0, 0), (0, 0), (1, 1), (0, 0)))
    zeroed = jnp.zeros(extent + (channels,), jnp.float32)
    input_grad = spread_taps(bordered[0], filters_full, extent, zeroed, False).astype(jnp.bfloat16)
    features = bordered[1]
    tap_list = []
    for p in range(3):
        for q in range(3):
            for r in range(3):
                window = features[p : p + extent[0], q : q + extent[1], r : r + extent[2]]
                tap_list.append(
                    jnp.einsum(
                        "xyzi,xyzo->io", window, grad_out, preferred_element_type=jnp.float32
                    )
                )
    partial_taps = jnp.stack(tap_list).reshape(3, 3, 3, channels, channels)
    across = lax.psum_scatter(partial_taps, "grp", scatter_dimension=3, tiled=True)
    taps_grad = lax.psum_scatter(across, "chan", scatter_dimension=4, tiled=True)
    halves = input_grad.reshape(extent[0] // 2, 2, extent[1] // 2, 2, extent[2] // 2, 2, channels)
    coarse = jnp.einsum(
        "iajbkcd,abced->jike", halves, upsample_weight, preferred_element_type=jnp.float32
    ).astype(jnp.bfloat16)
    coarse_extent = coarse.shape[:3]
    wide = filters_half.shape[3]
    slab = lax.all_to_all(coarse, "chan", split_axis=3, concat_axis=0, tiled=True)
    slab = padded_2(slab, (("grp", 1),), 1)
    slab = jnp.pad(slab, ((1, 1), (0, 0), (1, 1), (0, 0)))
    count = lax.axis_size("chan") * coarse_extent[0]
    blank = jnp.zeros((count, coarse_extent[1], coarse_extent[2], wide), jnp.float32)
    result = lax.psum_scatter(
        spread_taps(slab, filters_half, (count, coarse_extent[1], coarse_extent[2]), blank, True),
        "chan",
        scatter_dimension=0,
        tiled=True,
    )
    grad_half = result.astype(jnp.bfloat16)
    return (grad_half, taps_grad)


def solution(mesh):
    in_specs = (
        P("grp", "chan", None, None),
        P("grp", "chan", None, None),
        P(),
        P(),
        P(None, None, None, None, "chan"),
    )
    out_specs = (P("chan", "grp", None, None), P(None, None, None, "grp", "chan"))
    return jax.shard_map(body, mesh=mesh, in_specs=in_specs, out_specs=out_specs, check_vma=False)
```

profile of v0, /device:TPU:0, one launch (start us, length us, event | category | flops | bytes accessed | tf_op | source)
XLA Modules:
  0.0 166.8 jit_solution(15116668181056318444)
XLA Ops:
  7.2 0.9 pad_maximum_fusion.2
  8.1 4.9 %collective-permute-start = (bf16[2,1,2,16,128]{4,3,2,1,0:T(8,128)(2,1)S(1)}, bf16[2,1,2,16,128]{4,3,2,1,0:T(8,128)(2,1)S(1)}, u32[]{:S(2)}, u32[]{:S(2)}) collective-permute-start(bf16[2,1,2,16,128]{4,3,2,1,0:T(8,128)(2,1)S(1)} %get-tuple-element.6), channel_id=1, source_target_pairs={{0,4},{4,8},{8,12},{12,16},{16,20},{20,24},{24,28},{1,5},{5,9},{9,... | collective-permute-start | bytes 49160 | tf_op jit(solution)/shard_map/ppermute | solution.py:15
  13.0 1.3 collective-permute-start.1
  14.4 4.2 %collective-permute-done.1 = bf16[2,1,2,16,128]{4,3,2,1,0:T(8,128)(2,1)S(1)} collective-permute-done((bf16[2,1,2,16,128]{4,3,2,1,0:T(8,128)(2,1)S(1)}, bf16[2,1,2,16,128]{4,3,2,1,0:T(8,128)(2,1)S(1)}, u32[]{:S(2)}, u32[]{:S(2)}) %collective-permute-start.1) | collective-permute-done | bytes 16416 | tf_op jit(solution)/shard_map/ppermute | solution.py:17
  18.6 0.9 pad_maximum_fusion
  19.5 1.3 collective-permute-start.2
  20.8 1.3 collective-permute-start.3
  22.1 3.6 %collective-permute-done.3 = bf16[2,10,1,16,128]{4,3,2,1,0:T(8,128)(2,1)S(1)} collective-permute-done((bf16[2,10,1,16,128]{4,3,2,1,0:T(8,128)(2,1)S(1)}, bf16[2,10,1,16,128]{4,3,2,1,0:T(8,128)(2,1)S(1)}, u32[]{:S(2)}, u32[]{:S(2)}) %collective-permute-start.3) | collective-permute-done | bytes 81952 | tf_op jit(solution)/shard_map/ppermute | solution.py:17
  25.7 1.1 select_maximum_fusion
  31.5 0.4 fusion.37
  31.9 0.3 copy.12
  32.2 1.1 reshape.101
  33.3 4.4 %all-to-all-start = ((bf16[4,2,2048]{2,1,0:T(2,128)(2,1)}), bf16[4,2,2048]{2,1,0:T(2,128)(2,1)S(1)}, u32[]{:S(2)}, u32[]{:S(2)}) async-start(bf16[4,2,2048]{2,1,0:T(2,128)(2,1)} %reshape.101), calls=%async_computation | async-start | bytes 65536 | tf_op jit(solution)/shard_map/all_to_all | solution.py:66
  37.9 0.2 fusion.34
  38.1 0.2 fusion.33
  38.3 0.2 fusion.32
  38.5 0.2 fusion.31
  38.7 0.2 fusion.30
  38.9 0.2 fusion.29
  39.1 0.2 fusion.28
  39.3 0.2 fusion.27
  39.5 0.2 fusion.26
  39.7 0.2 fusion.25
  39.9 0.2 fusion.24
  40.1 0.2 fusion.23
  40.3 0.2 fusion.22
  40.5 0.2 fusion.21
  40.7 0.2 fusion.20
  40.9 0.2 fusion.19
  41.2 0.2 fusion.18
  41.4 0.2 fusion.17
  41.6 0.2 fusion.16
  41.8 0.2 fusion.15
  42.0 0.2 fusion.14
  42.2 0.2 fusion.13
  42.4 0.2 fusion.12
  42.6 0.2 fusion.11
  42.8 0.2 fusion.10
  43.0 0.2 fusion.9
  43.2 1.2 copy-done.2
  44.5 0.6 reshape.102
  45.2 0.2 copy.14
  45.4 4.3 %collective-permute-start.4 = (bf16[4,1,8,128]{3,2,1,0:T(8,128)(2,1)S(1)}, bf16[4,1,8,128]{3,2,1,0:T(8,128)(2,1)S(1)}, u32[]{:S(2)}, u32[]{:S(2)}) collective-permute-start(bf16[4,1,8,128]{3,2,1,0:T(8,128)(2,1)S(1)} %get-tuple-element.8), channel_id=1, source_target_pairs={{0,4},{4,8},{8,12},{12,16},{16,20},{20,24},{24,28},{1,5},{5,9},{9,... | collective-permute-start | bytes 24584 | tf_op jit(solution)/shard_map/ppermute | solution.py:15
  49.7 1.6 collective-permute-start.5
  51.3 1.1 fusion.71
  52.4 3.1 %collective-permute-done.5 = bf16[4,1,8,128]{3,2,1,0:T(8,128)(2,1)S(1)} collective-permute-done((bf16[4,1,8,128]{3,2,1,0:T(8,128)(2,1)S(1)}, bf16[4,1,8,128]{3,2,1,0:T(8,128)(2,1)S(1)}, u32[]{:S(2)}, u32[]{:S(2)}) %collective-permute-start.5) | collective-permute-done | bytes 8224 | tf_op jit(solution)/shard_map/ppermute | solution.py:17
  55.6 1.1 fusion.59
  56.7 1.1 fusion.61
  57.8 1.1 fusion.63
  58.9 1.1 fusion.65
  60.0 1.1 fusion.69
  61.1 1.1 fusion.73
  62.2 1.1 fusion.87
  65.3 0.2 fusion.7
  65.7 0.2 fusion.6
  66.9 0.9 convolution_add_fusion.2
  67.9 46.4 %reduce-scatter.8.cloned.1.call-done = f32[3,3,3,16,128]{4,3,2,1,0:T(8,128)} async-done(((f32[3,3,3,128,128]{4,3,2,1,0:T(8,128)}), f32[3,3,3,16,128]{4,3,2,1,0:T(8,128)}) %reduce-scatter.8.cloned.1.call-update) | async-done | bytes 221200 | tf_op jit(solution)/shard_map/reduce_scatter | solution.py:58
  114.3 2.5 %copy.99 = f32[3,3,3,16,128]{3,2,1,0,4:T(4,128)S(1)} copy(f32[3,3,3,16,128]{4,3,2,1,0:T(8,128)} %reduce-scatter.8.cloned.1.call-done) | data formatting | bytes 442368
  116.8 1.7 %reshape.99 = f32[128,432]{1,0:T(8,128)} reshape(f32[128,3,3,3,16]{4,3,2,1,0:T(4,128)S(1)} %bitcast.656) | data formatting | bytes 442368
  118.5 17.2 %reduce-scatter.6.cloned.1.call-done = f32[1,4,8,512]{3,2,1,0:T(8,128)} async-done(((f32[4,4,8,512]{3,2,1,0:T(8,128)}), f32[1,4,8,512]{3,2,1,0:T(8,128)}) %reduce-scatter.6.cloned.1.call-update) | async-done | bytes 65552 | tf_op jit(solution)/shard_map/reduce_scatter | solution.py:71
  135.7 1.5 convert_element_type.27
  137.2 21.1 %reduce-scatter.10.cloned.1.call-done = f32[32,432]{1,0:T(8,128)} async-done(((f32[128,432]{1,0:T(8,128)}), f32[32,432]{1,0:T(8,128)}) %reduce-scatter.10.cloned.1.call-update) | async-done | bytes 55312
  158.3 1.1 reshape.100
  159.4 0.9 copy.100
  (67 shorter events, 8.1 us)
Async XLA Ops:
  7.2 24.3 %copy-start = (bf16[2,2,2,512,128]{4,3,2,1,0:T(8,128)(2,1)S(1)}, bf16[2,2,2,512,128]{4,3,2,1,0:T(8,128)(2,1)}, u32[]{:S(2)}) copy-start(bf16[2,2,2,512,128]{4,3,2,1,0:T(8,128)(2,1)} %param.8) | copy-start | bytes 3145732
  7.2 19.7 %copy-start.3 = (bf16[3,3,3,128,128]{4,3,2,1,0:T(8,128)(2,1)S(1)}, bf16[3,3,3,128,128]{4,3,2,1,0:T(8,128)(2,1)}, u32[]{:S(2)}) copy-start(bf16[3,3,3,128,128]{4,3,2,1,0:T(8,128)(2,1)} %param.7) | copy-start | bytes 2654212
  8.1 6.3 %collective-permute-start = (bf16[2,1,2,16,128]{4,3,2,1,0:T(8,128)(2,1)S(1)}, bf16[2,1,2,16,128]{4,3,2,1,0:T(8,128)(2,1)S(1)}, u32[]{:S(2)}, u32[]{:S(2)}) collective-permute-start(bf16[2,1,2,16,128]{4,3,2,1,0:T(8,128)(2,1)S(1)} %get-tuple-element.6), channel_id=1, source_target_pairs={{0,4},{4,8},{8,12},{12,16},{16,20},{20,24},{24,28},{1,5},{5,9},{9,... | collective-permute-start | bytes 49160 | tf_op jit(solution)/shard_map/ppermute | solution.py:15
  13.0 5.6 %collective-permute-start.1 = (bf16[2,1,2,16,128]{4,3,2,1,0:T(8,128)(2,1)S(1)}, bf16[2,1,2,16,128]{4,3,2,1,0:T(8,128)(2,1)S(1)}, u32[]{:S(2)}, u32[]{:S(2)}) collective-permute-start(bf16[2,1,2,16,128]{4,3,2,1,0:T(8,128)(2,1)S(1)} %get-tuple-element.7), channel_id=1, source_target_pairs={{4,0},{8,4},{12,8},{16,12},{20,16},{24,20},{28,24},{5,1},{9,5},{13... | collective-permute-start | bytes 49160 | tf_op jit(solution)/shard_map/ppermute | solution.py:17
  19.5 2.6 %collective-permute-start.2 = (bf16[2,10,1,16,128]{4,3,2,1,0:T(8,128)(2,1)S(1)}, bf16[2,10,1,16,128]{4,3,2,1,0:T(8,128)(2,1)S(1)}, u32[]{:S(2)}, u32[]{:S(2)}) collective-permute-start(bf16[2,10,1,16,128]{4,3,2,1,0:T(8,128)(2,1)S(1)} %get-tuple-element.4), channel_id=1, source_target_pairs={{0,1},{1,2},{2,3},{4,5},{5,6},{6,7},{8,9},{9,10},{10,11},{12,13},{... | collective-permute-start | bytes 245768 | tf_op jit(solution)/shard_map/ppermute | solution.py:15
  20.8 4.9 %collective-permute-start.3 = (bf16[2,10,1,16,128]{4,3,2,1,0:T(8,128)(2,1)S(1)}, bf16[2,10,1,16,128]{4,3,2,1,0:T(8,128)(2,1)S(1)}, u32[]{:S(2)}, u32[]{:S(2)}) collective-permute-start(bf16[2,10,1,16,128]{4,3,2,1,0:T(8,128)(2,1)S(1)} %get-tuple-element.5), channel_id=1, source_target_pairs={{1,0},{2,1},{3,2},{5,4},{6,5},{7,6},{9,8},{10,9},{11,10},{13,12},{... | collective-permute-start | bytes 245768 | tf_op jit(solution)/shard_map/ppermute | solution.py:17
  31.3 6.4 %copy-start.4 = (bf16[8,2,16,128]{3,2,1,0:T(8,128)(2,1)S(1)}, bf16[8,2,16,128]{3,2,1,0:T(8,128)(2,1)}, u32[]{:S(2)}) copy-start(bf16[8,2,16,128]{3,2,1,0:T(8,128)(2,1)} %param.5) | copy-start | bytes 196612
  33.3 11.2 %all-to-all-start = ((bf16[4,2,2048]{2,1,0:T(2,128)(2,1)}), bf16[4,2,2048]{2,1,0:T(2,128)(2,1)S(1)}, u32[]{:S(2)}, u32[]{:S(2)}) async-start(bf16[4,2,2048]{2,1,0:T(2,128)(2,1)} %reshape.101), calls=%async_computation | async-start | bytes 65536 | tf_op jit(solution)/shard_map/all_to_all | solution.py:66
  37.7 76.6 %reduce-scatter.8.cloned.1.call-start = ((), (), s32[]{:S(2)}) async-start(), calls=%async_computation.5 | async-start | bytes 1990656 | tf_op jit(solution)/shard_map/reduce_scatter | solution.py:58
  43.2 1.3 copy-start.2
  44.5 91.3 %reduce-scatter.6.cloned.1.call-start = ((), (), s32[]{:S(2)}) async-start(), calls=%async_computation.4 | async-start | bytes 327680 | tf_op jit(solution)/shard_map/reduce_scatter | solution.py:71
  45.4 7.0 %collective-permute-start.4 = (bf16[4,1,8,128]{3,2,1,0:T(8,128)(2,1)S(1)}, bf16[4,1,8,128]{3,2,1,0:T(8,128)(2,1)S(1)}, u32[]{:S(2)}, u32[]{:S(2)}) collective-permute-start(bf16[4,1,8,128]{3,2,1,0:T(8,128)(2,1)S(1)} %get-tuple-element.8), channel_id=1, source_target_pairs={{0,4},{4,8},{8,12},{12,16},{16,20},{20,24},{24,28},{1,5},{5,9},{9,... | collective-permute-start | bytes 24584 | tf_op jit(solution)/shard_map/ppermute | solution.py:15
  49.7 13.6 %copy-start.1 = (bf16[3,3,3,512,128]{4,3,2,1,0:T(8,128)(2,1)S(1)}, bf16[3,3,3,512,128]{4,3,2,1,0:T(8,128)(2,1)}, u32[]{:S(2)}) copy-start(bf16[3,3,3,512,128]{4,3,2,1,0:T(8,128)(2,1)} %param.9) | copy-start | bytes 10616836
  49.7 5.8 %collective-permute-start.5 = (bf16[4,1,8,128]{3,2,1,0:T(8,128)(2,1)S(1)}, bf16[4,1,8,128]{3,2,1,0:T(8,128)(2,1)S(1)}, u32[]{:S(2)}, u32[]{:S(2)}) collective-permute-start(bf16[4,1,8,128]{3,2,1,0:T(8,128)(2,1)S(1)} %get-tuple-element.9), channel_id=1, source_target_pairs={{4,0},{8,4},{12,8},{16,12},{20,16},{24,20},{28,24},{5,1},{9,5},{13... | collective-permute-start | bytes 24584 | tf_op jit(solution)/shard_map/ppermute | solution.py:17
  67.9 90.4 %reduce-scatter.10.cloned.1.call-start = ((), (), s32[]{:S(2)}) async-start(), calls=%async_computation.6 | async-start | bytes 327680
Sparse Core Ops, SparseCore 0:
  44.6 69.6 reduce-scatter.7
  116.8 18.9 reduce-scatter.5
  138.2 20.0 reduce-scatter.9
where the time goes:
time: 168 us; the launch traced here: 167 us
  waiting for transfers between devices  95.8 us (57%)
  matrix products  23.3 us (14%)
  starting transfers between devices  19.1 us (11%)
  between operations  14.4 us (9%)
  local copies, waits for them, and re-layouts  9.76 us (6%)
  other arithmetic  4.41 us (3%)
    reduce_scatter x1, waiting for transfers between devices, body(): lax.psum_scatter(partial_taps, 'grp', scatter_dimension=3, tiled=True)  46.4 us
    unnamed x4, waiting for transfers between devices  21.1 us
    dot_general x54, matrix products, spread_taps(): jnp.einsum('xyzo,io->xyzi', window, kernel, preferred_element_type=jnp.fl...  17.5 us
    reduce_scatter x1, waiting for transfers between devices, body(): lax.psum_scatter(spread_taps(slab, filters_half, (count, coarse_extent[1]...  17.2 us
    ppermute x3, waiting for transfers between devices, padded_2(): lax.ppermute(head, axis, [((i + 1) % count, i) for i in range(ends)])  10.9 us
    ppermute x3, starting transfers between devices, padded_2(): lax.ppermute(tail, axis, [(i, (i + 1) % count) for i in range(ends)])  10.5 us
    unnamed x16, local copies, waits for them, and re-layouts  9.16 us
    dot_general x27, matrix products, body(): jnp.einsum('xyzi,xyzo->io', window, grad_out, preferred_element_type=jnp....  5.4 us
  transfers between devices with their start and end apart: 10, of which 7 were waited for; matrix products, arithmetic and copies ran while one was open for 15% of the time, Pallas kernels for 0%

commit v1 on v0

v1 whole, which is shorter than its diff:
```python
import jax
import jax.numpy as jnp
from jax import lax
from jax.experimental import pallas as pl
from jax.experimental.pallas import tpu as pltpu
from jax.sharding import PartitionSpec as P

F32 = jnp.float32
BF16 = jnp.bfloat16
NT = (((1,), (1,)), ((), ()))
NN = (((1,), (0,)), ((), ()))


def dot(a, b, dims):
    return lax.dot_general(a, b, dims, preferred_element_type=F32)


def partner(i, k, n):
    return i ^ k if n & (n - 1) == 0 else (k - i) % n


def swap(value, axis, k):
    n = lax.axis_size(axis)
    return lax.ppermute(value, axis, [(i, partner(i, k, n)) for i in range(n)])


def shift(value, axis, step):
    n = lax.axis_size(axis)
    return lax.ppermute(value, axis, [(i, (i + step) % n) for i in range(n)])


def pair(k, n):
    c = lax.axis_index("chan")
    return jnp.bitwise_xor(c, k) if n & (n - 1) == 0 else lax.rem(k - c + n, n)


def coarse_kernel(n, *refs):
    bricks, (full_ref, up_ref, own_ref, left_ref, right_ref, stage, spread) = refs[:n], refs[n:]
    nx, ny, nz, ch = bricks[0].shape
    rows, half_x, half_z = n * ny, nx // 2, nz // 2
    half_y = rows // 2
    width = own_ref.shape[3]
    spread[:, :, 0] = jnp.zeros((4, half_x, nz, ch), BF16)
    spread[:, :, rows + 1] = jnp.zeros((4, half_x, nz, ch), BF16)
    level = lax.broadcasted_iota(jnp.int32, (nx * ny, half_z, ch), 1)
    for k in range(n):
        stage[...] = bricks[k][...].astype(F32).reshape(nx * ny, nz, ch)
        even = stage[:, pl.ds(0, half_z, stride=2), :]
        odd = stage[:, pl.ds(1, half_z, stride=2), :]
        after = jnp.where(level == half_z - 1, 0.0, pltpu.roll(even, half_z - 1, 1))
        before = jnp.where(level == 0, 0.0, pltpu.roll(odd, 1, 1))
        first = pair(k, n) * ny + 1
        for which, value in enumerate((even, after, odd, before)):
            value = value.reshape(half_x, 2, ny, half_z, ch)
            for b in range(ny):
                packed = jnp.concatenate([value[:, 0, b], value[:, 1, b]], axis=1)
                spread[which, :, first + b] = packed.astype(BF16)
    taps = jnp.concatenate(
        [
            jnp.concatenate([full_ref[p, q, r] for q in range(3) for r in range(3)], axis=1)
            for p in range(3)
        ],
        axis=0,
    )
    grads = []
    for order in ((2, 0, 3), (1, 2, 0)):
        window = jnp.concatenate(
            [
                spread[which, :, 2 - q : 2 - q + rows].reshape(half_x * rows * nz, ch)
                for q in range(3)
                for which in order
            ],
            axis=1,
        )
        product = dot(window, taps, NT).reshape(half_x, rows, 2, half_z, 3 * ch)
        planes = {}
        for u in range(-1, nx + 1):
            terms = [
                product[x // 2, :, x % 2, :, p * ch : (p + 1) * ch]
                for p in range(3)
                for x in (u - p + 1,)
                if 0 <= x < nx
            ]
            total = terms[0]
            for term in terms[1:]:
                total = total + term
            planes[u] = total.reshape(half_y, 2, half_z, ch)
        grads.append(planes)
    nothing = jnp.zeros((half_y * half_z, ch), F32)
    columns = []
    for a in range(2):
        for b in range(2):
            for c in range(2):
                pieces = []
                for i in range(-1, half_x + 1):
                    u = 2 * i + a
                    inside = -1 <= u <= nx
                    pieces.append(
                        grads[c][u][:, b].reshape(half_y * half_z, ch) if inside else nothing
                    )
                columns.append(jnp.concatenate(pieces, axis=0).astype(BF16))
    start = pl.multiple_of(lax.axis_index("chan") * width, width)
    up = jnp.concatenate(
        [
            up_ref[a, b, c, pl.ds(start, width), :]
            for a in range(2)
            for b in range(2)
            for c in range(2)
        ],
        axis=1,
    )
    coarse = dot(jnp.concatenate(columns, axis=1), up, NT)
    coarse = coarse.reshape(half_x + 2, half_y, half_z, width)
    own_ref[...] = coarse
    left_ref[...] = coarse[:2]
    right_ref[...] = coarse[half_x:]


def half_kernel(n, m, own_ref, left_ref, right_ref, half_ref, *refs):
    outs, (padded, result) = refs[:n], refs[n:]
    wide_x, half_y, half_z, width = own_ref.shape
    half_x = wide_x - 2
    inputs = half_ref.shape[3]
    g = lax.axis_index("grp")
    low = jnp.where(g > 0, 1.0, 0.0)
    high = jnp.where(g < m - 1, 1.0, 0.0)
    planes = [own_ref[i] for i in range(wide_x)]
    planes[0] = (planes[0] + left_ref[0]) * low
    planes[1] = planes[1] + left_ref[1] * low
    planes[half_x] = planes[half_x] + right_ref[0] * high
    planes[half_x + 1] = (planes[half_x + 1] + right_ref[1]) * high
    padded[:, 0] = jnp.zeros((3, wide_x, half_z, width), F32)
    padded[:, half_y + 1] = jnp.zeros((3, wide_x, half_z, width), F32)
    level = lax.broadcasted_iota(jnp.int32, (half_y, half_z, width), 1)
    for i in range(wide_x):
        plane = planes[i].astype(BF16).astype(F32)
        padded[0, 1 : half_y + 1, i] = jnp.where(
            level == half_z - 1, 0.0, pltpu.roll(plane, half_z - 1, 1)
        )
        padded[1, 1 : half_y + 1, i] = plane
        padded[2, 1 : half_y + 1, i] = jnp.where(level == 0, 0.0, pltpu.roll(plane, 1, 1))
    cells = half_y * half_x * half_z
    total = None
    for p in range(3):
        windows = [
            padded[r, 2 - q : 2 - q + half_y, 2 - p : 2 - p + half_x]
            .reshape(cells, width)
            .astype(BF16)
            for q in range(3)
            for r in range(3)
        ]
        kernels = [half_ref[p, q, r] for q in range(3) for r in range(3)]
        if width % 128 == 0:
            windows = [jnp.concatenate(windows, axis=1)]
            kernels = [jnp.concatenate(kernels, axis=1)]
        for window, kernel in zip(windows, kernels):
            product = dot(window, kernel, NT)
            total = product if total is None else total + product
    share = half_y // n
    result[...] = total.reshape(n, share, half_x, half_z, inputs)
    for k in range(n):
        outs[k][...] = result[pair(k, n)].astype(outs[k].dtype)


def taps_kernel(n, m, *refs):
    grads, feats, (edge_ref, keep_ref, send_ref, spread, table) = (
        refs[:n],
        refs[n : 2 * n],
        refs[2 * n :],
    )
    nx, ny, nz, ch = grads[0].shape
    rows = n * ny
    part = ch // n
    block = ch // m
    spread[:, 0] = jnp.zeros((nx + 1, nz, ch), BF16)
    spread[:, rows + 1] = jnp.zeros((nx + 1, nz, ch), BF16)
    start = lax.axis_index("chan") * part
    source = lax.broadcasted_iota(jnp.int32, (ch, ch), 0)
    target = lax.broadcasted_iota(jnp.int32, (ch, ch), 1)
    copies = (lax.rem(target, part) + start == source) & (target < 3 * part)
    pick = jnp.where(copies, 1.0, 0.0).astype(BF16)
    bits = m.bit_length() - 1
    owner = source // block
    turned = jnp.zeros_like(owner)
    for bit in range(bits):
        turned = turned + (owner // 2**bit % 2) * 2 ** (bits - 1 - bit)
    order = jnp.where(turned * block + lax.rem(source, block) == target, 1.0, 0.0).astype(BF16)
    keep_edge = jnp.where(lax.axis_index("grp") > 0, 1.0, 0.0)
    flipped = {}
    for k in range(n):
        edge_grad = (edge_ref[k].astype(F32) * keep_edge).astype(BF16)
        edge_feat = (edge_ref[n + k].astype(F32) * keep_edge).astype(BF16)
        cells = jnp.concatenate([edge_grad[None], grads[k][...]], axis=0)
        cells = cells.reshape((nx + 1) * ny * nz, ch)
        chosen = dot(cells, pick, NN)
        level = lax.rem(lax.broadcasted_iota(jnp.int32, chosen.shape, 0), nz)
        lane = lax.broadcasted_iota(jnp.int32, chosen.shape, 1)
        count = chosen.shape[0]
        above = jnp.where(level == nz - 1, 0.0, pltpu.roll(chosen, count - 1, 0))
        below = jnp.where(level == 0, 0.0, pltpu.roll(chosen, 1, 0))
        mixed = jnp.where(lane < part, above, jnp.where(lane < 2 * part, chosen, below))
        mixed = mixed.astype(BF16).reshape(nx + 1, ny, nz, ch)
        first = pair(k, n) * ny + 1
        for b in range(ny):
            spread[:, first + b] = mixed[:, b]
        flipped[k] = jnp.concatenate([edge_feat[None], feats[k][...]], axis=0)
    base = None
    totals = []
    for p in range(3):
        totals.append(None)
    for p in range(3):
        grad_from = 1 if p < 2 else 0
        feat_from = 0 if p == 0 else 1
        total = None
        for k in range(n):
            first = pair(k, n) * ny
            feat = flipped[k][feat_from : feat_from + nx].reshape(nx * ny * nz, ch)
            feat = dot(order, feat, (((0,), (1,)), ((), ()))).astype(BF16)
            window = jnp.concatenate(
                [
                    spread[grad_from : grad_from + nx, pl.ds(first + 2 - q, ny)].reshape(
                        nx * ny * nz, ch
                    )
                    for q in range(3)
                ],
                axis=1,
            )
            product = dot(feat, window, NN)
            total = product if total is None else total + product
        for q in range(3):
            at = (3 * p + q) * ch
            table[:, at : at + ch] = total[:, q * ch : (q + 1) * ch]
    half = ch // 2
    bit = lax.rem(lax.axis_index("grp"), 2)
    keep_ref[...] = table[pl.ds(pl.multiple_of(bit * half, half), half), :]
    send_ref[...] = table[pl.ds(pl.multiple_of((1 - bit) * half, half), half), :].astype(BF16)


def finish_kernel(keep_ref, got_ref, out_ref):
    part = out_ref.shape[4]
    ch = keep_ref.shape[1] // 9
    total = keep_ref[...] + got_ref[...].astype(F32)
    for p in range(3):
        for q in range(3):
            for r in range(3):
                at = (3 * p + q) * ch + r * part
                out_ref[p, q, r] = total[:, at : at + part]


def call(kernel, outs, scratch):
    return pl.pallas_call(kernel, out_shape=outs, scratch_shapes=scratch)


def body(grad_out, feat_full, filters_full, upsample_weight, filters_half):
    n, m = lax.axis_size("chan"), lax.axis_size("grp")
    nx, ny, nz, ch = grad_out.shape
    half_x, half_y, half_z = nx // 2, n * ny // 2, nz // 2
    width = filters_half.shape[4]
    shape = jax.ShapeDtypeStruct
    grads = [grad_out] + [swap(grad_out, "chan", k) for k in range(1, n)]
    feats = [feat_full] + [swap(feat_full, "chan", k) for k in range(1, n)]
    edges = jnp.stack([v[nx - 1] for v in grads] + [v[nx - 1] for v in feats])
    edges = shift(edges, "grp", 1)
    border = shape((2, half_y, half_z, width), F32)
    own, left, right = call(
        lambda *refs: coarse_kernel(n, *refs),
        [shape((half_x + 2, half_y, half_z, width), F32), border, border],
        [
            pltpu.VMEM((nx * ny, nz, ch), F32),
            pltpu.VMEM((4, half_x, n * ny + 2, nz, ch), BF16),
        ],
    )(*grads, filters_full, upsample_weight)
    from_left = shift(right, "grp", 1)
    from_right = shift(left, "grp", -1)
    keep, send = call(
        lambda *refs: taps_kernel(n, m, *refs),
        [shape((ch // 2, 9 * ch), F32), shape((ch // 2, 9 * ch), BF16)],
        [
            pltpu.VMEM((nx + 1, n * ny + 2, nz, ch), BF16),
            pltpu.VMEM((ch, 9 * ch), F32),
        ],
    )(*grads, *feats, edges)
    chunk = (half_y // n, half_x, half_z, filters_half.shape[3])
    chunks = call(
        lambda *refs: half_kernel(n, m, *refs),
        [shape(chunk, F32)] + [shape(chunk, BF16)] * (n - 1),
        [
            pltpu.VMEM((3, half_y + 2, half_x + 2, half_z, width), F32),
            pltpu.VMEM((n,) + chunk, F32),
        ],
    )(own, from_left, from_right, filters_half)
    grad_half = chunks[0]
    for k in range(1, n):
        grad_half = grad_half + swap(chunks[k], "chan", k).astype(F32)
    grad_half = grad_half.astype(BF16)
    got = swap(send, "grp", 1)
    for bit in range(1, m.bit_length() - 1):
        total = keep + got.astype(F32)
        half = total.shape[0] // 2
        upper = lax.rem(lax.div(lax.axis_index("grp"), 2**bit), 2) == 1
        keep = jnp.where(upper, total[half:], total[:half])
        send = jnp.where(upper, total[:half], total[half:]).astype(BF16)
        got = swap(send, "grp", 2**bit)
    taps_grad = call(finish_kernel, shape((3, 3, 3, ch // m, ch // n), F32), [])(keep, got)
    return (grad_half, taps_grad)


def solution(mesh):
    in_specs = (
        P("grp", "chan", None, None),
        P("grp", "chan", None, None),
        P(),
        P(),
        P(None, None, None, None, "chan"),
    )
    out_specs = (P("chan", "grp", None, None), P(None, None, None, "grp", "chan"))
    return jax.shard_map(body, mesh=mesh, in_specs=in_specs, out_specs=out_specs, check_vma=False)
```

time: 168 us -> 52.1 us (0.31)
  waiting for transfers between devices: 95.8 us -> 18.3 us
  matrix products: 23.3 us -> 0 us
  between operations: 14.4 us -> 0.73 us
  Pallas kernels: 0 us -> 13.5 us
  local copies, waits for them, and re-layouts: 9.76 us -> 3.35 us
  starting transfers between devices: 19.1 us -> 13.6 us
  other arithmetic: 4.41 us -> 2.19 us
    reduce_scatter x2 -> x0, waiting for transfers between devices: 63.6 us -> none  [the longest x1 46.4 us: body(): lax.psum_scatter(partial_taps, 'grp', scatter_dimension=3, tiled=True)]
    dot_general x82 -> x0, matrix products: 23.3 us -> none  [the longest x54 17.5 us: spread_taps(): jnp.einsum('xyzo,io->xyzi', window, kernel, preferred_element_type=jnp.fl...]
    unnamed x4 -> x0, waiting for transfers between devices: 21.1 us -> none
    pallas_call x0 -> x4, Pallas kernels: none -> 13.5 us  [the longest x1 4.23 us: body(): call(lambda *refs: coarse_kernel(n, *refs), [shape((half_x + 2, half_y, h...]
    ppermute x6 -> x15, waiting for transfers between devices: 11.1 us -> 18.3 us  [the longest x12 10.8 us: swap(): return lax.ppermute(value, axis, [(i, partner(i, k, n)) for i in range(n)])]
    unnamed x16 -> x29, local copies, waits for them, and re-layouts: 9.16 us -> 3.34 us
    all_to_all x1 -> x0, starting transfers between devices: 4.36 us -> none  [body(): lax.all_to_all(coarse, 'chan', split_axis=3, concat_axis=0, tiled=True)]
    concatenate x3 -> x0, other arithmetic: 2.06 us -> none  [padded_2(): jnp.concatenate([lax.ppermute(tail, axis, [(i, (i + 1) % count) for i in...]
  transfers between devices with their start and end apart: 10 -> 15, of which waited for: 7 -> 9; matrix products, arithmetic and copies ran while one was open for 15% -> 7% of each run, Pallas kernels for 0% -> 16%
where the time goes in v1:
time: 52.1 us; the launch traced here: 51.7 us
  waiting for transfers between devices  18.3 us (35%)
  starting transfers between devices  13.6 us (26%)
  Pallas kernels  13.5 us (26%)
  local copies, waits for them, and re-layouts  3.35 us (6%)
  other arithmetic  2.19 us (4%)
  between operations  0.73 us (1%)
    ppermute x12, waiting for transfers between devices, swap(): return lax.ppermute(value, axis, [(i, partner(i, k, n)) for i in range(n)])  10.8 us
    ppermute x3, waiting for transfers between devices, shift(): return lax.ppermute(value, axis, [(i, (i + step) % n) for i in range(n)])  7.54 us
    ppermute x12, starting transfers between devices, swap(): return lax.ppermute(value, axis, [(i, partner(i, k, n)) for i in range(n)])  7.32 us
    ppermute x3, starting transfers between devices, shift(): return lax.ppermute(value, axis, [(i, (i + step) % n) for i in range(n)])  6.24 us
    pallas_call x1, Pallas kernels, body(): call(lambda *refs: coarse_kernel(n, *refs), [shape((half_x + 2, half_y, h...  4.23 us
    pallas_call x1, Pallas kernels, body(): call(lambda *refs: half_kernel(n, m, *refs), [shape(chunk, F32)] + [shape...  4.04 us
    pallas_call x1, Pallas kernels, body(): call(lambda *refs: taps_kernel(n, m, *refs), [shape((ch // 2, 9 * ch), F3...  3.57 us
    unnamed x29, local copies, waits for them, and re-layouts  3.34 us
  transfers between devices with their start and end apart: 15, of which 9 were waited for; matrix products, arithmetic and copies ran while one was open for 7% of the time, Pallas kernels for 16%

profile of v1, /device:TPU:0, one launch (start us, length us, event | category | flops | bytes accessed | tf_op | source)
XLA Modules:
  0.0 51.7 jit_solution(14426990556179028166)
XLA Ops:
  0.6 0.6 %collective-permute-start = (bf16[8,2,16,128]{3,2,1,0:T(8,128)(2,1)}, bf16[8,2,16,128]{3,2,1,0:T(8,128)(2,1)S(1)}, u32[]{:S(2)}, u32[]{:S(2)}) collective-permute-start(bf16[8,2,16,128]{3,2,1,0:T(8,128)(2,1)} %refs_0_.3), channel_id=1, source_target_pairs={{0,1},{1,0},{2,3},{3,2},{4,5},{5,4},{6,7},{7,6},{8,9},{9,8},{10,11... | collective-permute-start | bytes 196616 | tf_op jit(solution)/shard_map/ppermute | solution.py:24
  1.2 2.6 %collective-permute-start.1 = (bf16[8,2,16,128]{3,2,1,0:T(8,128)(2,1)}, bf16[8,2,16,128]{3,2,1,0:T(8,128)(2,1)S(1)}, u32[]{:S(2)}, u32[]{:S(2)}) collective-permute-start(bf16[8,2,16,128]{3,2,1,0:T(8,128)(2,1)} %refs_0_.3), channel_id=1, source_target_pairs={{0,2},{1,3},{2,0},{3,1},{4,6},{5,7},{6,4},{7,5},{8,10},{9,11},{10,... | collective-permute-start | bytes 196616 | tf_op jit(solution)/shard_map/ppermute | solution.py:24
  3.7 0.0 collective-permute-start.2
  3.8 0.2 collective-permute-start.8
  3.9 1.9 %collective-permute-start.9 = (bf16[8,2,16,128]{3,2,1,0:T(8,128)(2,1)}, bf16[8,2,16,128]{3,2,1,0:T(8,128)(2,1)S(1)}, u32[]{:S(2)}, u32[]{:S(2)}) collective-permute-start(bf16[8,2,16,128]{3,2,1,0:T(8,128)(2,1)} %refs_4_.3), channel_id=1, source_target_pairs={{0,2},{1,3},{2,0},{3,1},{4,6},{5,7},{6,4},{7,5},{8,10},{9,11},{10,... | collective-permute-start | bytes 196616 | tf_op jit(solution)/shard_map/ppermute | solution.py:24
  5.9 0.7 %constant_dynamic-update-slice_fusion.7 = bf16[8,2,16,128]{3,2,1,0:T(8,128)(2,1)S(1)} fusion(bf16[8,2,16,128]{3,2,1,0:T(8,128)(2,1)} %refs_0_.3), kind=kLoop, calls=%fused_computation.13 | loop fusion | bytes 16384
  6.6 0.0 collective-permute-done.refs_1_
  6.6 0.0 copy-start
  6.6 0.0 collective-permute-start.10
  6.6 0.0 collective-permute-done.1.refs_2_
  6.6 0.0 copy-start.1
  6.6 1.4 %collective-permute-done.2.refs_3_ = bf16[8,2,16,128]{3,2,1,0:T(8,128)(2,1)S(1)} collective-permute-done((bf16[8,2,16,128]{3,2,1,0:T(8,128)(2,1)}, bf16[8,2,16,128]{3,2,1,0:T(8,128)(2,1)S(1)}, u32[]{:S(2)}, u32[]{:S(2)}) %collective-permute-start.2) | collective-permute-done | bytes 65568 | tf_op jit(solution)/shard_map/ppermute | solution.py:24
  8.0 0.0 copy-start.2
  8.0 0.7 %constant_dynamic-update-slice_fusion.3 = bf16[8,2,16,128]{3,2,1,0:T(8,128)(2,1)S(1)} fusion(bf16[8,2,16,128]{3,2,1,0:T(8,128)(2,1)S(1)} %constant_dynamic-update-slice_fusion.4, bf16[8,2,16,128]{3,2,1,0:T(8,128)(2,1)} %refs_4_.3), kind=kLoop, calls=%fused_computation.9 | loop fusion | bytes 16384
  8.8 0.0 collective-permute-done.8.refs_5_
  8.8 0.0 copy-start.4
  8.8 1.0 %collective-permute-done.9.refs_6_ = bf16[8,2,16,128]{3,2,1,0:T(8,128)(2,1)S(1)} collective-permute-done((bf16[8,2,16,128]{3,2,1,0:T(8,128)(2,1)}, bf16[8,2,16,128]{3,2,1,0:T(8,128)(2,1)S(1)}, u32[]{:S(2)}, u32[]{:S(2)}) %collective-permute-start.9) | collective-permute-done | bytes 65568 | tf_op jit(solution)/shard_map/ppermute | solution.py:24
  9.8 0.0 copy-start.5
  9.8 1.4 %collective-permute-done.10.refs_7_ = bf16[8,2,16,128]{3,2,1,0:T(8,128)(2,1)S(1)} collective-permute-done((bf16[8,2,16,128]{3,2,1,0:T(8,128)(2,1)}, bf16[8,2,16,128]{3,2,1,0:T(8,128)(2,1)S(1)}, u32[]{:S(2)}, u32[]{:S(2)}) %collective-permute-start.10) | collective-permute-done | bytes 65568 | tf_op jit(solution)/shard_map/ppermute | solution.py:24
  11.1 0.0 copy-start.6
  11.2 1.5 %collective-permute-start.11 = (bf16[8,2,16,128]{3,2,1,0:T(8,128)(2,1)S(1)}, bf16[8,2,16,128]{3,2,1,0:T(8,128)(2,1)S(1)}, u32[]{:S(2)}, u32[]{:S(2)}) collective-permute-start(bf16[8,2,16,128]{3,2,1,0:T(8,128)(2,1)S(1)} %constant_dynamic-update-slice_fusion), channel_id=1, source_target_pairs={{0,4},{4,8},{8,12},{12,16},{16,20},{20,24},{24,28},{28,0},{1,5},{5... | collective-permute-start | bytes 196616 | tf_op jit(solution)/shard_map/ppermute | solution.py:29
  12.7 5.4 %collective-permute-done.11.refs_8_ = bf16[8,2,16,128]{3,2,1,0:T(8,128)(2,1)S(1)} collective-permute-done((bf16[8,2,16,128]{3,2,1,0:T(8,128)(2,1)S(1)}, bf16[8,2,16,128]{3,2,1,0:T(8,128)(2,1)S(1)}, u32[]{:S(2)}, u32[]{:S(2)}) %collective-permute-start.11) | collective-permute-done | bytes 65568 | tf_op jit(solution)/shard_map/ppermute | solution.py:29
  18.1 0.0 copy-done
  18.1 0.0 copy-done.1
  18.1 0.0 copy-done.2
  18.1 0.0 copy-done.4
  18.1 0.0 copy-done.5
  18.1 0.0 copy-done.6
  18.2 0.0 copy-start.7
  18.2 0.6 %copy-done.7 = bf16[8,2,16,128]{3,2,1,0:T(8,128)(2,1)} copy-done((bf16[8,2,16,128]{3,2,1,0:T(8,128)(2,1)}, bf16[8,2,16,128]{3,2,1,0:T(8,128)(2,1)S(1)}, u32[]{:S(2)}) %copy-start.7) | copy-done | bytes 65560
  18.8 3.6 %shard_map.70 = (f32[64,1152]{1,0:T(8,128)}, bf16[64,1152]{1,0:T(8,128)(2,1)}) custom-call(bf16[8,2,16,128]{3,2,1,0:T(8,128)(2,1)} %refs_0_.3, bf16[8,2,16,128]{3,2,1,0:T(8,128)(2,1)} %copy-done, bf16[8,2,16,128]{3,2,1,0:T(8,128)(2,1)} %copy-done.1, bf16[8,2,16,128]{3,2,1,0:T(8,128)(2,1)} %copy-done.2, bf16[8,2,16,128]{3,2,1,0:T(8,128)(2,1)} %refs_4_.3, ...), custom_call_target="tpu_custom_call" | custom-call | tf_op jit(solution)/shard_map/pallas_call | solution.py:275
  22.4 0.0 copy-start.3
  22.4 0.0 collective-permute-start.12
  22.4 4.2 %shard_map.68 = (f32[6,4,8,128]{3,2,1,0:T(8,128)}, f32[2,4,8,128]{3,2,1,0:T(8,128)}, f32[2,4,8,128]{3,2,1,0:T(8,128)}) custom-call(bf16[8,2,16,128]{3,2,1,0:T(8,128)(2,1)} %refs_0_.3, bf16[8,2,16,128]{3,2,1,0:T(8,128)(2,1)} %copy-done, bf16[8,2,16,128]{3,2,1,0:T(8,128)(2,1)} %copy-done.1, bf16[8,2,16,128]{3,2,1,0:T(8,128)(2,1)} %copy-done.2, ...), custom_call_target="tpu_custom_call" | custom-call | tf_op jit(solution)/shard_map/pallas_call | solution.py:265
  26.6 2.0 %collective-permute-start.3 = (f32[2,4,8,128]{3,2,1,0:T(8,128)}, f32[2,4,8,128]{3,2,1,0:T(8,128)S(1)}, u32[]{:S(2)}, u32[]{:S(2)}) collective-permute-start(f32[2,4,8,128]{3,2,1,0:T(8,128)} %get-tuple-element.12), channel_id=1, source_target_pairs={{0,4},{4,8},{8,12},{12,16},{16,20},{20,24},{24,28},{28,0},{1,5},{5... | collective-permute-start | bytes 98312 | tf_op jit(solution)/shard_map/ppermute | solution.py:29
  28.6 2.7 %collective-permute-start.4 = (f32[2,4,8,128]{3,2,1,0:T(8,128)}, f32[2,4,8,128]{3,2,1,0:T(8,128)S(1)}, u32[]{:S(2)}, u32[]{:S(2)}) collective-permute-start(f32[2,4,8,128]{3,2,1,0:T(8,128)} %get-tuple-element.13), channel_id=1, source_target_pairs={{0,28},{4,0},{8,4},{12,8},{16,12},{20,16},{24,20},{28,24},{1,29},{... | collective-permute-start | bytes 98312 | tf_op jit(solution)/shard_map/ppermute | solution.py:29
  31.3 2.1 %collective-permute-done.3.refs_1_ = f32[2,4,8,128]{3,2,1,0:T(8,128)S(1)} collective-permute-done((f32[2,4,8,128]{3,2,1,0:T(8,128)}, f32[2,4,8,128]{3,2,1,0:T(8,128)S(1)}, u32[]{:S(2)}, u32[]{:S(2)}) %collective-permute-start.3) | collective-permute-done | bytes 32800 | tf_op jit(solution)/shard_map/ppermute | solution.py:29
  33.4 0.0 copy-start.9
  33.4 0.0 collective-permute-done.4.refs_2_
  33.4 0.0 copy-start.10
  33.4 0.6 %copy-done.9 = f32[2,4,8,128]{3,2,1,0:T(8,128)} copy-done((f32[2,4,8,128]{3,2,1,0:T(8,128)}, f32[2,4,8,128]{3,2,1,0:T(8,128)S(1)}, u32[]{:S(2)}) %copy-start.9) | copy-done | bytes 32792
  34.0 0.0 copy-done.10
  34.0 4.0 %shard_map.69 = (f32[1,4,8,512]{3,2,1,0:T(8,128)}, bf16[1,4,8,512]{3,2,1,0:T(8,128)(2,1)}, bf16[1,4,8,512]{3,2,1,0:T(8,128)(2,1)}, bf16[1,4,8,512]{3,2,1,0:T(8,128)(2,1)}) custom-call(f32[6,4,8,128]{3,2,1,0:T(8,128)} %get-tuple-element.11.refs_0_, f32[2,4,8,128]{3,2,1,0:T(8,128)} %copy-done.9, f32[2,4,8,128]{3,2,1,0:T(8,128)} %copy-done.10, ...), custom_call_target="tpu_custom_call" | custom-call | tf_op jit(solution)/shard_map/pallas_call | solution.py:284
  38.1 0.0 collective-permute-start.7
  38.1 1.1 %collective-permute-start.6 = (bf16[1,4,8,512]{3,2,1,0:T(8,128)(2,1)}, bf16[1,4,8,512]{3,2,1,0:T(8,128)(2,1)S(1)}, u32[]{:S(2)}, u32[]{:S(2)}) collective-permute-start(bf16[1,4,8,512]{3,2,1,0:T(8,128)(2,1)} %get-tuple-element.16), channel_id=1, source_target_pairs={{0,2},{1,3},{2,0},{3,1},{4,6},{5,7},{6,4},{7,5},{8,10},{9,11},{10,... | collective-permute-start | bytes 98312 | tf_op jit(solution)/shard_map/ppermute | solution.py:24
  39.2 0.7 %collective-permute-start.5 = (bf16[1,4,8,512]{3,2,1,0:T(8,128)(2,1)}, bf16[1,4,8,512]{3,2,1,0:T(8,128)(2,1)S(1)}, u32[]{:S(2)}, u32[]{:S(2)}) collective-permute-start(bf16[1,4,8,512]{3,2,1,0:T(8,128)(2,1)} %get-tuple-element.15), channel_id=1, source_target_pairs={{0,1},{1,0},{2,3},{3,2},{4,5},{5,4},{6,7},{7,6},{8,9},{9,8},{10,11... | collective-permute-start | bytes 98312 | tf_op jit(solution)/shard_map/ppermute | solution.py:24
  39.9 0.0 collective-permute-done.12
  39.9 0.0 copy-done.3
  40.0 0.1 collective-permute-start.13
  40.1 1.6 %collective-permute-done.7 = bf16[1,4,8,512]{3,2,1,0:T(8,128)(2,1)S(1)} collective-permute-done((bf16[1,4,8,512]{3,2,1,0:T(8,128)(2,1)}, bf16[1,4,8,512]{3,2,1,0:T(8,128)(2,1)S(1)}, u32[]{:S(2)}, u32[]{:S(2)}) %collective-permute-start.7) | collective-permute-done | bytes 32800 | tf_op jit(solution)/shard_map/ppermute | solution.py:24
  41.6 0.7 %collective-permute-done.6 = bf16[1,4,8,512]{3,2,1,0:T(8,128)(2,1)S(1)} collective-permute-done((bf16[1,4,8,512]{3,2,1,0:T(8,128)(2,1)}, bf16[1,4,8,512]{3,2,1,0:T(8,128)(2,1)S(1)}, u32[]{:S(2)}, u32[]{:S(2)}) %collective-permute-start.6) | collective-permute-done | bytes 32800 | tf_op jit(solution)/shard_map/ppermute | solution.py:24
  42.3 0.0 collective-permute-done.5
  42.3 1.5 %add_convert_fusion = bf16[1,4,8,512]{3,2,1,0:T(8,128)(2,1)} fusion(bf16[1,4,8,512]{3,2,1,0:T(8,128)(2,1)S(1)} %collective-permute-done.7, bf16[1,4,8,512]{3,2,1,0:T(8,128)(2,1)S(1)} %collective-permute-done.6, f32[1,4,8,512]{3,2,1,0:T(8,128)} %get-tuple-element.14, bf16[1,4,8,512]{3,2,1,0:T(8,128)(2,1)S(1)} %collective-permute-done.5), kind=kLoop, calls=%fused_computation.5 | loop fusion | flops 114688 | bytes 196608 | tf_op jit(solution)/shard_map/convert_element_type | solution.py:295
  43.8 0.6 %collective-permute-done.13 = bf16[32,1152]{1,0:T(8,128)(2,1)S(1)} collective-permute-done((bf16[32,1152]{1,0:T(8,128)(2,1)S(1)}, bf16[32,1152]{1,0:T(8,128)(2,1)S(1)}, u32[]{:S(2)}, u32[]{:S(2)}) %collective-permute-start.13) | collective-permute-done | bytes 73760 | tf_op jit(solution)/shard_map/ppermute | solution.py:24
  44.5 0.1 collective-permute-start.14
  44.6 0.6 %slice_select_fusion.keep_ref = f32[16,1152]{1,0:T(8,128)} fusion(f32[32,1152]{1,0:T(8,128)S(1)} %convert_add_fusion.1, pred[]{:T(512)S(6)} %eq.6), kind=kLoop, calls=%fused_computation.4 | loop fusion | flops 18432 | bytes 221185 | tf_op jit(solution)/shard_map/jit(_where)/select_n | solution.py:301
  45.2 4.2 %collective-permute-done.14.got_ref = bf16[16,1152]{1,0:T(8,128)(2,1)S(1)} collective-permute-done((bf16[16,1152]{1,0:T(8,128)(2,1)S(1)}, bf16[16,1152]{1,0:T(8,128)(2,1)S(1)}, u32[]{:S(2)}, u32[]{:S(2)}) %collective-permute-start.14) | collective-permute-done | bytes 36896 | tf_op jit(solution)/shard_map/ppermute | solution.py:24
  49.4 0.0 copy-start.8
  49.4 0.6 %copy-done.8 = bf16[16,1152]{1,0:T(8,128)(2,1)} copy-done((bf16[16,1152]{1,0:T(8,128)(2,1)}, bf16[16,1152]{1,0:T(8,128)(2,1)S(1)}, u32[]{:S(2)}) %copy-start.8) | copy-done | bytes 36888
  50.0 1.7 %shard_map.71 = f32[3,3,3,16,32]{4,3,2,1,0:T(8,128)} custom-call(f32[16,1152]{1,0:T(8,128)} %slice_select_fusion.keep_ref, bf16[16,1152]{1,0:T(8,128)(2,1)} %copy-done.8), custom_call_target="tpu_custom_call" | custom-call | tf_op jit(solution)/shard_map/pallas_call | solution.py:304
  (10 shorter events, 0.1 us)
Async XLA Ops:
  0.6 6.0 %collective-permute-start = (bf16[8,2,16,128]{3,2,1,0:T(8,128)(2,1)}, bf16[8,2,16,128]{3,2,1,0:T(8,128)(2,1)S(1)}, u32[]{:S(2)}, u32[]{:S(2)}) collective-permute-start(bf16[8,2,16,128]{3,2,1,0:T(8,128)(2,1)} %refs_0_.3), channel_id=1, source_target_pairs={{0,1},{1,0},{2,3},{3,2},{4,5},{5,4},{6,7},{7,6},{8,9},{9,8},{10,11... | collective-permute-start | bytes 196616 | tf_op jit(solution)/shard_map/ppermute | solution.py:24
  1.2 5.4 %collective-permute-start.1 = (bf16[8,2,16,128]{3,2,1,0:T(8,128)(2,1)}, bf16[8,2,16,128]{3,2,1,0:T(8,128)(2,1)S(1)}, u32[]{:S(2)}, u32[]{:S(2)}) collective-permute-start(bf16[8,2,16,128]{3,2,1,0:T(8,128)(2,1)} %refs_0_.3), channel_id=1, source_target_pairs={{0,2},{1,3},{2,0},{3,1},{4,6},{5,7},{6,4},{7,5},{8,10},{9,11},{10,... | collective-permute-start | bytes 196616 | tf_op jit(solution)/shard_map/ppermute | solution.py:24
  3.7 4.3 %collective-permute-start.2 = (bf16[8,2,16,128]{3,2,1,0:T(8,128)(2,1)}, bf16[8,2,16,128]{3,2,1,0:T(8,128)(2,1)S(1)}, u32[]{:S(2)}, u32[]{:S(2)}) collective-permute-start(bf16[8,2,16,128]{3,2,1,0:T(8,128)(2,1)} %refs_0_.3), channel_id=1, source_target_pairs={{0,3},{1,2},{2,1},{3,0},{4,7},{5,6},{6,5},{7,4},{8,11},{9,10},{10,... | collective-permute-start | bytes 196616 | tf_op jit(solution)/shard_map/ppermute | solution.py:24
  3.8 5.0 %collective-permute-start.8 = (bf16[8,2,16,128]{3,2,1,0:T(8,128)(2,1)}, bf16[8,2,16,128]{3,2,1,0:T(8,128)(2,1)S(1)}, u32[]{:S(2)}, u32[]{:S(2)}) collective-permute-start(bf16[8,2,16,128]{3,2,1,0:T(8,128)(2,1)} %refs_4_.3), channel_id=1, source_target_pairs={{0,1},{1,0},{2,3},{3,2},{4,5},{5,4},{6,7},{7,6},{8,9},{9,8},{10,11... | collective-permute-start | bytes 196616 | tf_op jit(solution)/shard_map/ppermute | solution.py:24
  3.9 5.8 %collective-permute-start.9 = (bf16[8,2,16,128]{3,2,1,0:T(8,128)(2,1)}, bf16[8,2,16,128]{3,2,1,0:T(8,128)(2,1)S(1)}, u32[]{:S(2)}, u32[]{:S(2)}) collective-permute-start(bf16[8,2,16,128]{3,2,1,0:T(8,128)(2,1)} %refs_4_.3), channel_id=1, source_target_pairs={{0,2},{1,3},{2,0},{3,1},{4,6},{5,7},{6,4},{7,5},{8,10},{9,11},{10,... | collective-permute-start | bytes 196616 | tf_op jit(solution)/shard_map/ppermute | solution.py:24
  6.6 11.5 %copy-start = (bf16[8,2,16,128]{3,2,1,0:T(8,128)(2,1)}, bf16[8,2,16,128]{3,2,1,0:T(8,128)(2,1)S(1)}, u32[]{:S(2)}) copy-start(bf16[8,2,16,128]{3,2,1,0:T(8,128)(2,1)S(1)} %collective-permute-done.refs_1_) | copy-start | bytes 196612
  6.6 4.6 %collective-permute-start.10 = (bf16[8,2,16,128]{3,2,1,0:T(8,128)(2,1)}, bf16[8,2,16,128]{3,2,1,0:T(8,128)(2,1)S(1)}, u32[]{:S(2)}, u32[]{:S(2)}) collective-permute-start(bf16[8,2,16,128]{3,2,1,0:T(8,128)(2,1)} %refs_4_.3), channel_id=1, source_target_pairs={{0,3},{1,2},{2,1},{3,0},{4,7},{5,6},{6,5},{7,4},{8,11},{9,10},{10,... | collective-permute-start | bytes 196616 | tf_op jit(solution)/shard_map/ppermute | solution.py:24
  6.6 11.5 %copy-start.1 = (bf16[8,2,16,128]{3,2,1,0:T(8,128)(2,1)}, bf16[8,2,16,128]{3,2,1,0:T(8,128)(2,1)S(1)}, u32[]{:S(2)}) copy-start(bf16[8,2,16,128]{3,2,1,0:T(8,128)(2,1)S(1)} %collective-permute-done.1.refs_2_) | copy-start | bytes 196612
  8.0 10.1 %copy-start.2 = (bf16[8,2,16,128]{3,2,1,0:T(8,128)(2,1)}, bf16[8,2,16,128]{3,2,1,0:T(8,128)(2,1)S(1)}, u32[]{:S(2)}) copy-start(bf16[8,2,16,128]{3,2,1,0:T(8,128)(2,1)S(1)} %collective-permute-done.2.refs_3_) | copy-start | bytes 196612
  8.8 9.4 %copy-start.4 = (bf16[8,2,16,128]{3,2,1,0:T(8,128)(2,1)}, bf16[8,2,16,128]{3,2,1,0:T(8,128)(2,1)S(1)}, u32[]{:S(2)}) copy-start(bf16[8,2,16,128]{3,2,1,0:T(8,128)(2,1)S(1)} %collective-permute-done.8.refs_5_) | copy-start | bytes 196612
  9.8 8.4 %copy-start.5 = (bf16[8,2,16,128]{3,2,1,0:T(8,128)(2,1)}, bf16[8,2,16,128]{3,2,1,0:T(8,128)(2,1)S(1)}, u32[]{:S(2)}) copy-start(bf16[8,2,16,128]{3,2,1,0:T(8,128)(2,1)S(1)} %collective-permute-done.9.refs_6_) | copy-start | bytes 196612
  11.1 7.0 %copy-start.6 = (bf16[8,2,16,128]{3,2,1,0:T(8,128)(2,1)}, bf16[8,2,16,128]{3,2,1,0:T(8,128)(2,1)S(1)}, u32[]{:S(2)}) copy-start(bf16[8,2,16,128]{3,2,1,0:T(8,128)(2,1)S(1)} %collective-permute-done.10.refs_7_) | copy-start | bytes 196612
  11.2 7.0 %collective-permute-start.11 = (bf16[8,2,16,128]{3,2,1,0:T(8,128)(2,1)S(1)}, bf16[8,2,16,128]{3,2,1,0:T(8,128)(2,1)S(1)}, u32[]{:S(2)}, u32[]{:S(2)}) collective-permute-start(bf16[8,2,16,128]{3,2,1,0:T(8,128)(2,1)S(1)} %constant_dynamic-update-slice_fusion), channel_id=1, source_target_pairs={{0,4},{4,8},{8,12},{12,16},{16,20},{20,24},{24,28},{28,0},{1,5},{5... | collective-permute-start | bytes 196616 | tf_op jit(solution)/shard_map/ppermute | solution.py:29
  18.2 0.6 %copy-start.7 = (bf16[8,2,16,128]{3,2,1,0:T(8,128)(2,1)}, bf16[8,2,16,128]{3,2,1,0:T(8,128)(2,1)S(1)}, u32[]{:S(2)}) copy-start(bf16[8,2,16,128]{3,2,1,0:T(8,128)(2,1)S(1)} %collective-permute-done.11.refs_8_) | copy-start | bytes 196612
  22.4 17.6 %copy-start.3 = (f32[64,1152]{1,0:T(8,128)S(1)}, f32[64,1152]{1,0:T(8,128)}, u32[]{:S(2)}) copy-start(f32[64,1152]{1,0:T(8,128)} %get-tuple-element.18) | copy-start | bytes 884740
  22.4 17.6 %collective-permute-start.12 = (bf16[64,1152]{1,0:T(8,128)(2,1)}, bf16[64,1152]{1,0:T(8,128)(2,1)S(1)}, u32[]{:S(2)}, u32[]{:S(2)}) collective-permute-start(bf16[64,1152]{1,0:T(8,128)(2,1)} %get-tuple-element.19), channel_id=1, source_target_pairs={{0,4},{4,0},{8,12},{12,8},{16,20},{20,16},{24,28},{28,24},{1,5},{5... | collective-permute-start | bytes 442376 | tf_op jit(solution)/shard_map/ppermute | solution.py:24
  26.6 6.8 %collective-permute-start.3 = (f32[2,4,8,128]{3,2,1,0:T(8,128)}, f32[2,4,8,128]{3,2,1,0:T(8,128)S(1)}, u32[]{:S(2)}, u32[]{:S(2)}) collective-permute-start(f32[2,4,8,128]{3,2,1,0:T(8,128)} %get-tuple-element.12), channel_id=1, source_target_pairs={{0,4},{4,8},{8,12},{12,16},{16,20},{20,24},{24,28},{28,0},{1,5},{5... | collective-permute-start | bytes 98312 | tf_op jit(solution)/shard_map/ppermute | solution.py:29
  28.6 4.8 %collective-permute-start.4 = (f32[2,4,8,128]{3,2,1,0:T(8,128)}, f32[2,4,8,128]{3,2,1,0:T(8,128)S(1)}, u32[]{:S(2)}, u32[]{:S(2)}) collective-permute-start(f32[2,4,8,128]{3,2,1,0:T(8,128)} %get-tuple-element.13), channel_id=1, source_target_pairs={{0,28},{4,0},{8,4},{12,8},{16,12},{20,16},{24,20},{28,24},{1,29},{... | collective-permute-start | bytes 98312 | tf_op jit(solution)/shard_map/ppermute | solution.py:29
  33.4 0.6 %copy-start.9 = (f32[2,4,8,128]{3,2,1,0:T(8,128)}, f32[2,4,8,128]{3,2,1,0:T(8,128)S(1)}, u32[]{:S(2)}) copy-start(f32[2,4,8,128]{3,2,1,0:T(8,128)S(1)} %collective-permute-done.3.refs_1_) | copy-start | bytes 98308
  33.4 0.6 %copy-start.10 = (f32[2,4,8,128]{3,2,1,0:T(8,128)}, f32[2,4,8,128]{3,2,1,0:T(8,128)S(1)}, u32[]{:S(2)}) copy-start(f32[2,4,8,128]{3,2,1,0:T(8,128)S(1)} %collective-permute-done.4.refs_2_) | copy-start | bytes 98308
  38.1 3.6 %collective-permute-start.7 = (bf16[1,4,8,512]{3,2,1,0:T(8,128)(2,1)}, bf16[1,4,8,512]{3,2,1,0:T(8,128)(2,1)S(1)}, u32[]{:S(2)}, u32[]{:S(2)}) collective-permute-start(bf16[1,4,8,512]{3,2,1,0:T(8,128)(2,1)} %get-tuple-element.17), channel_id=1, source_target_pairs={{0,3},{1,2},{2,1},{3,0},{4,7},{5,6},{6,5},{7,4},{8,11},{9,10},{10,... | collective-permute-start | bytes 98312 | tf_op jit(solution)/shard_map/ppermute | solution.py:24
  38.1 4.3 %collective-permute-start.6 = (bf16[1,4,8,512]{3,2,1,0:T(8,128)(2,1)}, bf16[1,4,8,512]{3,2,1,0:T(8,128)(2,1)S(1)}, u32[]{:S(2)}, u32[]{:S(2)}) collective-permute-start(bf16[1,4,8,512]{3,2,1,0:T(8,128)(2,1)} %get-tuple-element.16), channel_id=1, source_target_pairs={{0,2},{1,3},{2,0},{3,1},{4,6},{5,7},{6,4},{7,5},{8,10},{9,11},{10,... | collective-permute-start | bytes 98312 | tf_op jit(solution)/shard_map/ppermute | solution.py:24
  39.2 3.1 %collective-permute-start.5 = (bf16[1,4,8,512]{3,2,1,0:T(8,128)(2,1)}, bf16[1,4,8,512]{3,2,1,0:T(8,128)(2,1)S(1)}, u32[]{:S(2)}, u32[]{:S(2)}) collective-permute-start(bf16[1,4,8,512]{3,2,1,0:T(8,128)(2,1)} %get-tuple-element.15), channel_id=1, source_target_pairs={{0,1},{1,0},{2,3},{3,2},{4,5},{5,4},{6,7},{7,6},{8,9},{9,8},{10,11... | collective-permute-start | bytes 98312 | tf_op jit(solution)/shard_map/ppermute | solution.py:24
  40.0 4.4 %collective-permute-start.13 = (bf16[32,1152]{1,0:T(8,128)(2,1)S(1)}, bf16[32,1152]{1,0:T(8,128)(2,1)S(1)}, u32[]{:S(2)}, u32[]{:S(2)}) collective-permute-start(bf16[32,1152]{1,0:T(8,128)(2,1)S(1)} %select_convert_fusion), channel_id=1, source_target_pairs={{0,8},{4,12},{8,0},{12,4},{16,24},{20,28},{24,16},{28,20},{1,9},{5... | collective-permute-start | bytes 221192 | tf_op jit(solution)/shard_map/ppermute | solution.py:24
  44.5 4.9 %collective-permute-start.14 = (bf16[16,1152]{1,0:T(8,128)(2,1)S(1)}, bf16[16,1152]{1,0:T(8,128)(2,1)S(1)}, u32[]{:S(2)}, u32[]{:S(2)}) collective-permute-start(bf16[16,1152]{1,0:T(8,128)(2,1)S(1)} %select_convert_fusion.1), channel_id=1, source_target_pairs={{0,16},{4,20},{8,24},{12,28},{16,0},{20,4},{24,8},{28,12},{1,17},{... | collective-permute-start | bytes 110600 | tf_op jit(solution)/shard_map/ppermute | solution.py:24
  49.4 0.6 %copy-start.8 = (bf16[16,1152]{1,0:T(8,128)(2,1)}, bf16[16,1152]{1,0:T(8,128)(2,1)S(1)}, u32[]{:S(2)}) copy-start(bf16[16,1152]{1,0:T(8,128)(2,1)S(1)} %collective-permute-done.14.got_ref) | copy-start | bytes 110596
